TPU v7x, 128 devices: a whole 4x4x4 slice. The times are simulated.
128 devices in a mesh: dp: 16 (over y, z), mp: 8 (over x, core).
Axes of the slice: x: 4, y: 4, z: 4, core: 2. Of those that a mesh axis runs over, the one named last changes fastest.
Arguments:
- hidden_in: bfloat16 [4096, 2304], P('dp'), may hold values from -6 to 6
- attn_gain: float32 [2304], replicated, may hold values from 0.25 to 1.75
- w_query: bfloat16 [2304, 2048], P(None, 'mp'), may hold values from -0.25 to 0.25
- w_key: bfloat16 [2304, 2048], P(None, 'mp'), may hold values from -0.125 to 0.125
- w_value: bfloat16 [2304, 2048], P(None, 'mp'), may hold values from -0.125 to 0.125
- w_out: bfloat16 [2048, 2304], P('mp'), may hold values from -0.5 to 0.5
- root_cache: bfloat16 [2, 4096, 2048], P(None, 'dp', 'mp'), may hold values from -400 to 400
- mid_cache: bfloat16 [2, 16, 1024, 2048], P(None, 'dp', None, 'mp'), may hold values from -400 to 400
- leaf_cache: bfloat16 [2, 32, 1024, 2048], P(None, 'dp', None, 'mp'), may hold values from -400 to 400
- mid_len: int32 [16], P('dp'), may hold values from 1 to 1024, 8192 in all
- leaf_len: int32 [32], P('dp'), may hold values from 1 to 1024, 16384 in all
- leaf_of: int32 [128], P('dp'), may hold values from 0 to 31, as said below
- parents: int32 [32], replicated, may hold values from 0 to 15, as said below
- suffix_len: int32 [128], P('dp'), may hold values from 1 to 32, 3072 in all
- ffn_gain: float32 [2304], replicated, may hold values from 0.25 to 1.75
- w_router: float32 [2304, 8], replicated, may hold values from -0.5 to 0.5
- routes: int32 [4096, 2], P('dp'), may hold values from 0 to 7, all different within a row; in each aligned block of 256 rows (0 to 255, 256 to 511, ...) at most 96 rows name the same one
- w_gate: bfloat16 [8, 2304, 5760], P('mp', None, 'dp'), may hold values from -0.125 to 0.125
- w_up: bfloat16 [8, 2304, 5760], P('mp', None, 'dp'), may hold values from -0.125 to 0.125
- w_down: bfloat16 [8, 5760, 2304], P('mp', 'dp'), may hold values from -0.078125 to 0.078125
Outputs:
- layer_out: bfloat16 [4096, 2304], P(('dp', 'mp'))
Inputs may be any that keep to these rules, and one draw needn't show every extreme that they name: `leaf_of`: leaf n belongs to index n // 2 of dp, mid-level node n to index n. The 8 sequences of one index of dp have different mid-level nodes and leaves of one parity, so that no two of them share a mid-level node or a leaf's owner. `parents`: every mid-level node is the parent of exactly one even and one odd leaf. `routes`: in the rows of one index of dp no expert is named by more than 96 rows; some indices of dp reach 96.
All inputs are finite; a program needn't handle non-finite values. No bound on the sum of `mid_len` or of `leaf_len` or of `suffix_len` on one device may be relied on, other than what follows from the above.
Results may differ from a plain program's by a relative error of at most 0.015.
The roundings to bfloat16 on the way count: a program that leaves them out, or rounds other values in their place, can miss the bound.
Values may be sent and summed in bfloat16 or wider, within the bound.
A program may use at most 128 MiB of HBM per device.

v0:
```python
import math
import jax
import jax.numpy as jnp
from jax import lax
from jax.sharding import PartitionSpec as P

HD = 64
TOP = 2
EPS = 1e-05
NEGATIVE = -1e30


def rms_scale(rows, gain):
    rows_wide = rows.astype(jnp.float32)
    mean_square = jnp.mean(rows_wide * rows_wide, axis=-1, keepdims=True)
    return rows_wide * lax.rsqrt(mean_square + EPS) * gain


def level_partial(queries, node_keys, node_values, limits, heads_here, batched):
    senders, row_count, width = queries.shape
    head_dim = width // heads_here
    scale = 1.0 / math.sqrt(head_dim)
    query_heads = queries.reshape(senders, row_count, heads_here, head_dim)
    if batched:
        key_heads = node_keys.reshape(senders, -1, heads_here, head_dim)
        value_heads = node_values.reshape(senders, -1, heads_here, head_dim)
        scores = jnp.einsum(
            "sqhd,skhd->sqhk", query_heads, key_heads, preferred_element_type=jnp.float32
        )
    else:
        key_heads = node_keys.reshape(-1, heads_here, head_dim)
        value_heads = node_values.reshape(-1, heads_here, head_dim)
        scores = jnp.einsum(
            "sqhd,khd->sqhk", query_heads, key_heads, preferred_element_type=jnp.float32
        )
    scores = scores * scale
    slots = jnp.arange(scores.shape[-1], dtype=jnp.int32)
    allowed = slots[None, :] < limits[:, None]
    scores = jnp.where(allowed[:, None, None, :], scores, NEGATIVE)
    peak = jnp.max(scores, axis=-1)
    weights = jnp.exp(scores - peak[..., None])
    total = jnp.sum(weights, axis=-1)
    probs = weights.astype(jnp.bfloat16)
    if batched:
        summed = jnp.einsum(
            "sqhk,skhd->sqhd", probs, value_heads, preferred_element_type=jnp.float32
        )
    else:
        summed = jnp.einsum(
            "sqhk,khd->sqhd", probs, value_heads, preferred_element_type=jnp.float32
        )
    result = (summed / total[..., None]).reshape(senders, row_count, width)
    return (result, peak + jnp.log(total))


def on_device(
    hidden_in,
    attn_gain,
    w_query,
    w_key,
    w_value,
    w_out,
    root_cache,
    mid_cache,
    leaf_cache,
    mid_len,
    leaf_len,
    leaf_of,
    parents,
    suffix_len,
    ffn_gain,
    w_router,
    routes,
    w_gate,
    w_up,
    w_down,
):
    tok_rows, width = hidden_in.shape
    seq_rows = suffix_len.shape[0]
    suffix = tok_rows // seq_rows
    head_dim = HD
    local_width = w_query.shape[1]
    heads_here = local_width // head_dim
    scale = 1.0 / math.sqrt(head_dim)
    owners = lax.axis_size("dp")
    normed = rms_scale(hidden_in, attn_gain).astype(jnp.bfloat16)
    query = jnp.dot(normed, w_query, preferred_element_type=jnp.float32).astype(jnp.bfloat16)
    key = jnp.dot(normed, w_key, preferred_element_type=jnp.float32).astype(jnp.bfloat16)
    value = jnp.dot(normed, w_value, preferred_element_type=jnp.float32).astype(jnp.bfloat16)
    query_heads = query.reshape(tok_rows, heads_here, head_dim)
    piece = lax.all_gather(root_cache, "dp", axis=1, tiled=True)
    running_peak = jnp.full((tok_rows, heads_here), NEGATIVE, jnp.float32)
    piece_keys = piece[0].reshape(-1, heads_here, head_dim)
    piece_values = piece[1].reshape(-1, heads_here, head_dim)
    scores = (
        jnp.einsum("qhd,khd->qhk", query_heads, piece_keys, preferred_element_type=jnp.float32)
        * scale
    )
    new_peak = jnp.maximum(running_peak, jnp.max(scores, axis=-1))
    weights = jnp.exp(scores - new_peak[..., None])
    new_total = jnp.sum(weights, axis=-1)
    added = jnp.einsum(
        "qhk,khd->qhd",
        weights.astype(jnp.bfloat16),
        piece_values,
        preferred_element_type=jnp.float32,
    )
    root_out = added / new_total[..., None]
    root_lse = new_peak + jnp.log(new_total)
    query_seq = query.reshape(seq_rows, suffix, heads_here, head_dim)
    key_seq = key.reshape(seq_rows, suffix, heads_here, head_dim)
    value_seq = value.reshape(seq_rows, suffix, heads_here, head_dim)
    slots = jnp.arange(suffix, dtype=jnp.int32)
    self_ok = (slots[None, None, :] <= slots[None, :, None]) & (
        slots[None, None, :] < suffix_len[:, None, None]
    )
    self_scores = (
        jnp.einsum("sqhd,skhd->sqhk", query_seq, key_seq, preferred_element_type=jnp.float32)
        * scale
    )
    self_scores = jnp.where(self_ok[:, :, None, :], self_scores, NEGATIVE)
    self_peak = jnp.max(self_scores, axis=-1)
    self_weights = jnp.exp(self_scores - self_peak[..., None])
    self_total = jnp.sum(self_weights, axis=-1)
    self_sum = jnp.einsum(
        "sqhk,skhd->sqhd",
        self_weights.astype(jnp.bfloat16),
        value_seq,
        preferred_element_type=jnp.float32,
    )
    self_out = (self_sum / self_total[..., None]).reshape(tok_rows, heads_here, head_dim)
    self_lse = (self_peak + jnp.log(self_total)).reshape(tok_rows, heads_here)
    mid_of = parents[leaf_of]
    leaf_owner = leaf_of // 2
    targets = jnp.arange(owners, dtype=jnp.int32)
    pick_mid = (mid_of[None, :] == targets[:, None]).astype(jnp.bfloat16)
    pick_leaf = (leaf_owner[None, :] == targets[:, None]).astype(jnp.bfloat16)
    flat_query = query.reshape(seq_rows, suffix * local_width)
    sent_mid = jnp.dot(pick_mid, flat_query, preferred_element_type=jnp.float32).astype(
        jnp.bfloat16
    )
    sent_leaf = jnp.dot(pick_leaf, flat_query, preferred_element_type=jnp.float32).astype(
        jnp.bfloat16
    )
    sent = jnp.stack([sent_mid, sent_leaf], axis=1).reshape(owners, 2, suffix, local_width)
    sent_queries = lax.all_to_all(sent, "dp", split_axis=0, concat_axis=0, tiled=True)
    leaf_every = lax.all_gather(leaf_of, "dp", axis=0, tiled=True).reshape(owners, seq_rows)
    me_dp = lax.axis_index("dp")
    second = jnp.any((leaf_every // 2 == me_dp) & (leaf_every % 2 == 1), axis=1)
    senders = sent_queries.shape[0]
    mid_limit = jnp.broadcast_to(mid_len[0], (senders,))
    mid_result, mid_logsum = level_partial(
        sent_queries[:, 0], mid_cache[0, 0], mid_cache[1, 0], mid_limit, heads_here, False
    )
    leaf_keys = jnp.where(second[:, None, None], leaf_cache[0, 1][None], leaf_cache[0, 0][None])
    leaf_values = jnp.where(second[:, None, None], leaf_cache[1, 1][None], leaf_cache[1, 0][None])
    leaf_limit = jnp.where(second, leaf_len[1], leaf_len[0])
    leaf_result, leaf_logsum = level_partial(
        sent_queries[:, 1], leaf_keys, leaf_values, leaf_limit, heads_here, True
    )
    owner_out = jnp.stack([mid_result, leaf_result], axis=1)
    owner_lse = jnp.stack([mid_logsum, leaf_logsum], axis=1)
    owner_all = jnp.concatenate([owner_out, owner_lse], axis=-1)
    back_all = lax.all_to_all(owner_all, "dp", split_axis=0, concat_axis=0, tiled=True)
    back_out = back_all[..., :local_width]
    back_lse = back_all[..., local_width:]
    mid_out = back_out[mid_of, 0].reshape(tok_rows, heads_here, head_dim)
    mid_lse = back_lse[mid_of, 0].reshape(tok_rows, heads_here)
    leaf_out = back_out[leaf_owner, 1].reshape(tok_rows, heads_here, head_dim)
    leaf_lse = back_lse[leaf_owner, 1].reshape(tok_rows, heads_here)
    stacked_lse = jnp.stack([root_lse, mid_lse, leaf_lse, self_lse])
    stacked_out = jnp.stack([root_out, mid_out, leaf_out, self_out])
    overall = jnp.max(stacked_lse, axis=0)
    shares = jnp.exp(stacked_lse - overall)
    combined = jnp.sum(shares[..., None] * stacked_out, axis=0) / jnp.sum(shares, axis=0)[..., None]
    attended = combined.reshape(tok_rows, local_width).astype(jnp.bfloat16)
    projected = jnp.dot(attended, w_out, preferred_element_type=jnp.float32)
    rows_here = tok_rows // lax.axis_size("mp")
    first = lax.axis_index("mp") * rows_here
    attn_rows = lax.psum_scatter(projected, "mp", scatter_dimension=0, tiled=True)
    resid = lax.dynamic_slice_in_dim(hidden_in, first, rows_here, 0).astype(jnp.float32) + attn_rows
    ffn_rows = rms_scale(resid, ffn_gain).astype(jnp.bfloat16)
    ffn_in = lax.all_gather(ffn_rows, "mp", axis=0, tiled=True)
    logits = jnp.dot(ffn_in.astype(jnp.float32), w_router, precision=lax.Precision.HIGHEST)
    chosen = jnp.take_along_axis(logits, routes, axis=1)
    squashed = jax.nn.sigmoid(chosen)
    gates = squashed / jnp.sum(squashed, axis=1, keepdims=True)
    expert = lax.axis_index("mp")
    hit_each = routes == expert
    hit = jnp.any(hit_each, axis=1)
    gate_here = jnp.sum(jnp.where(hit_each, gates, 0.0), axis=1)
    order = jnp.cumsum(hit.astype(jnp.int32)) - 1
    capacity = 3 * TOP * tok_rows // (2 * lax.axis_size("mp"))
    slot_ids = jnp.arange(capacity, dtype=jnp.int32)
    pick_slot = (order[None, :] == slot_ids[:, None]) & hit[None, :]
    dispatch = jnp.dot(
        pick_slot.astype(jnp.bfloat16), ffn_in, preferred_element_type=jnp.float32
    ).astype(jnp.bfloat16)
    slot_gate = jnp.dot(pick_slot.astype(jnp.float32), gate_here, precision=lax.Precision.HIGHEST)
    gate_weight = w_gate[0]
    up_weight = w_up[0]
    down_weight = w_down[0]
    piece = lax.all_gather(dispatch, "dp", axis=0, tiled=True)
    gate_part = jnp.dot(piece, gate_weight, preferred_element_type=jnp.float32)
    up_part = jnp.dot(piece, up_weight, preferred_element_type=jnp.float32)
    partial_out = jnp.dot(
        (jax.nn.silu(gate_part) * up_part).astype(jnp.bfloat16),
        down_weight,
        preferred_element_type=jnp.float32,
    )
    expert_out = lax.psum_scatter(
        partial_out.astype(jnp.bfloat16), "dp", scatter_dimension=0, tiled=True
    )
    weighted = expert_out.astype(jnp.float32) * slot_gate[:, None]
    spread = jnp.dot(pick_slot.astype(jnp.float32).T, weighted, precision=lax.Precision.HIGHEST)
    mixed = lax.psum_scatter(
        spread.astype(jnp.bfloat16), "mp", scatter_dimension=0, tiled=True
    ).astype(jnp.float32)
    row_ids = first + jnp.arange(rows_here, dtype=jnp.int32)
    valid = row_ids % suffix < suffix_len[row_ids // suffix]
    return jnp.where(valid[:, None], resid + mixed, 0.0).astype(jnp.bfloat16)


def solution(mesh):
    return jax.shard_map(
        on_device,
        mesh=mesh,
        in_specs=(
            P("dp", None),
            P(),
            P(None, "mp"),
            P(None, "mp"),
            P(None, "mp"),
            P("mp", None),
            P(None, "dp", "mp"),
            P(None, "dp", None, "mp"),
            P(None, "dp", None, "mp"),
            P("dp"),
            P("dp"),
            P("dp"),
            P(),
            P("dp"),
            P(),
            P(),
            P("dp", None),
            P("mp", None, "dp"),
            P("mp", None, "dp"),
            P("mp", "dp", None),
        ),
        out_specs=P(("dp", "mp"), None),
        check_vma=False,
    )
```

profile of v0, /device:TPU:0, one launch (start us, length us, event | category | flops | bytes accessed | tf_op | source)
XLA Modules:
  0.0 436.8 jit_solution(13475134126374077228)
XLA Ops:
  7.3 1.6 fusion.30
  9.6 2.4 convolution_convert_fusion.7
  14.9 8.2 %all-to-all-start = ((bf16[16,2,32,256]{3,2,1,0:T(8,128)(2,1)}), bf16[16,2,32,256]{3,2,1,0:T(8,128)(2,1)}, u32[]{:S(2)}, u32[]{:S(2)}) async-start(bf16[16,2,32,256]{3,2,1,0:T(8,128)(2,1)} %pad_maximum_fusion.1), calls=%async_computation | async-start | bytes 1048576 | tf_op jit(solution)/shard_map/all_to_all | solution.py:146
  24.6 17.4 %all-reduce.2 = s32[128]{0:T(128)S(1)} all-reduce(s32[128]{0:T(128)S(1)} %dynamic-update-slice), channel_id=1, replica_groups=mesh['dp'=16,'mp'=8] {'dp'}, use_global_device_ids=true, to_apply=%add.2 | all-reduce | flops 128 | bytes 1024
  42.9 1.3 broadcast_select_fusion
  44.9 2.2 fusion.126
  47.2 2.5 convolution_convert_fusion.6
  49.7 1.2 fusion.125
  53.8 2.1 copy.294
  56.0 2.1 copy.296
  60.2 2.0 fusion.129
  64.6 4.3 bitcast_reduce_fusion.1
  68.9 2.6 fusion.15
  71.6 2.7 fusion.58
  75.1 1.4 stack_reshape.23
  76.5 2.4 bitcast_reduce_fusion.2
  78.9 2.0 fusion.13
  80.9 1.8 fusion.63
  83.5 1.4 stack_reshape.22
  85.2 2.4 pad_maximum_fusion
  87.6 5.1 %all-to-all-start.1 = ((f32[16,2,32,260]{3,2,1,0:T(8,128)}), f32[16,2,32,260]{3,2,1,0:T(8,128)S(1)}, u32[]{:S(2)}, u32[]{:S(2)}) async-start(f32[16,2,32,260]{3,2,1,0:T(8,128)} %pad_maximum_fusion), calls=%async_computation.1 | async-start | bytes 3145728 | tf_op jit(solution)/shard_map/all_to_all | solution.py:164
  92.9 1.2 fusion.74
  94.3 2.8 convolution_convert_fusion.5
  98.2 1.4 fusion.45
  100.4 1.9 copy.288
  102.3 10.9 %all-to-all-done.1 = f32[16,2,32,260]{3,2,1,0:T(8,128)S(1)} async-done(((f32[16,2,32,260]{3,2,1,0:T(8,128)}), f32[16,2,32,260]{3,2,1,0:T(8,128)S(1)}, u32[]{:S(2)}, u32[]{:S(2)}) %all-to-all-start.1) | async-done | bytes 1064992 | tf_op jit(solution)/shard_map/all_to_all | solution.py:164
  114.1 1.3 copy.298
  118.0 1.8 gather_fusion.4
  119.8 1.8 gather_fusion.5
  122.5 4.5 %fusion.124 = (bf16[1,4096,256]{2,1,0:T(8,128)(2,1)}, bf16[1,4096,256]{2,1,0:T(8,128)(2,1)}) fusion(bf16[2,4096,256]{2,1,0:T(8,128)(2,1)} %all-gather.4.cloned.1.call-done), kind=kLoop, calls=%fused_computation.185 | loop fusion | bytes 8388608 | tf_op jit(solution)/shard_map/slice | solution.py:93
  127.0 4.1 copy.253
  131.1 4.2 copy.282
  135.2 9.7 %bitcast_reduce_fusion = (f32[256,4]{0,1:T(4,128)S(1)}, f32[4,256,4096]{2,1,0:T(8,128)}) fusion(bf16[256,4,64]{0,2,1:T(8,128)(2,1)S(1)} %bitcast.190, bf16[4096,4,64]{0,2,1:T(8,128)(2,1)} %bitcast.174), kind=kOutput, calls=%fused_computation.8 | convolution fusion | flops 545258496 | bytes 19009536 | tf_op jit(solution)/shard_map/qhd,khd->qhk/dot_general | solution.py:96
  144.9 8.6 %fusion.2 = f32[256,4]{0,1:T(4,128)S(1)} fusion(f32[4,256,4096]{2,1,0:T(8,128)} %get-tuple-element.33, f32[256,4]{0,1:T(4,128)S(1)} %broadcast_maximum_fusion), kind=kLoop, calls=%fused_computation.11 | loop fusion | flops 12581888 | bytes 16785408 | tf_op jit(solution)/shard_map/reduce_sum | solution.py:101
  153.6 8.1 %fusion.54 = f32[1,256,4,64]{1,3,2,0:T(8,128)S(1)} fusion(bf16[4096,4,64]{0,2,1:T(8,128)(2,1)} %bitcast.176, f32[4,256,4096]{2,1,0:T(8,128)} %get-tuple-element.33, f32[256,4]{0,1:T(4,128)S(1)} %broadcast_maximum_fusion, f32[256,4]{0,1:T(4,128)S(1)} %fusion.2), kind=kOutput, calls=%fused_computation.71 | convolution fusion | flops 549519360 | bytes 19144704 | tf_op jit(solution)/shard_map/qhk,khd->qhd/dot_general | solution.py:102
  163.0 1.9 fusion.130
  165.0 31.7 %reduce-scatter.4.cloned.1.call-done = f32[32,2304]{1,0:T(8,128)} async-done(((f32[256,2304]{1,0:T(8,128)}), f32[32,2304]{1,0:T(8,128)}) %reduce-scatter.4.cloned.1.call-update) | async-done | bytes 294928 | tf_op jit(solution)/shard_map/reduce_scatter | solution.py:180
  197.8 1.8 multiply_convert_fusion
  200.3 21.9 %all-gather.6.cloned.1.call-done = bf16[256,2304]{1,0:T(8,128)(2,1)} async-done(((bf16[32,2304]{1,0:T(8,128)(2,1)}), bf16[256,2304]{1,0:T(8,128)(2,1)}) %all-gather.6.cloned.1.call-update) | async-done | bytes 1179664 | tf_op jit(solution)/shard_map/all_gather | solution.py:183
  222.2 2.4 convolution_convert_fusion.4
  224.9 65.0 %all-gather.8.cloned.1.call-done = bf16[1536,2304]{1,0:T(8,128)(2,1)} async-done(((bf16[96,2304]{1,0:T(8,128)(2,1)}), bf16[1536,2304]{1,0:T(8,128)(2,1)}) %all-gather.8.cloned.1.call-update) | async-done | bytes 7077904 | tf_op jit(solution)/shard_map/all_gather | solution.py:203
  289.9 7.6 %fusion.35 = f32[1536,360]{0,1:T(8,128)} fusion(bf16[1536,2304]{1,0:T(8,128)(2,1)} %all-gather.8.cloned.1.call-done, bf16[1,2304,360]{1,2,0:T(8,128)(2,1)} %param.37), kind=kOutput, calls=%fused_computation.55 | convolution fusion | flops 2548039680 | bytes 10948608 | tf_op jit(solution)/shard_map/dot_general | solution.py:204
  297.5 13.1 %convolution_convert_fusion = bf16[1536,2304]{1,0:T(8,128)(2,1)} fusion(bf16[1,360,2304]{2,1,0:T(8,128)(2,1)S(1)} %copy-done, bf16[1536,2304]{1,0:T(8,128)(2,1)} %all-gather.8.cloned.1.call-done, f32[1536,360]{0,1:T(8,128)} %fusion.35, bf16[1,2304,360]{1,2,0:T(8,128)(2,1)} %param.38), kind=kOutput, calls=%fused_computation.12 | convolution fusion | flops 5102936064 | bytes 19685376 | tf_op jit(solution)/shard_map/dot_general | solution.py:206
  312.9 3.6 gather_fusion.6
  316.9 76.4 %reduce-scatter.6.cloned.1.call-done = bf16[96,2304]{1,0:T(8,128)(2,1)} async-done(((bf16[1536,2304]{1,0:T(8,128)(2,1)}), bf16[96,2304]{1,0:T(8,128)(2,1)}) %reduce-scatter.6.cloned.1.call-update) | async-done | bytes 442384 | tf_op jit(solution)/shard_map/reduce_scatter | solution.py:211
  393.3 3.2 convolution_convert_fusion.3
  397.3 30.7 %reduce-scatter.8.cloned.1.call-done = bf16[32,2304]{1,0:T(8,128)(2,1)} async-done(((bf16[256,2304]{1,0:T(8,128)(2,1)}), bf16[32,2304]{1,0:T(8,128)(2,1)}) %reduce-scatter.8.cloned.1.call-update) | async-done | bytes 147472 | tf_op jit(solution)/shard_map/reduce_scatter | solution.py:216
  428.0 1.7 select_convert_fusion
  (151 shorter events, 28.8 us)
Async XLA Ops:
  6.5 290.9 %copy-start = (bf16[1,360,2304]{2,1,0:T(8,128)(2,1)S(1)}, bf16[1,360,2304]{2,1,0:T(8,128)(2,1)}, u32[]{:S(2)}) copy-start(bf16[1,360,2304]{2,1,0:T(8,128)(2,1)} %param.39) | copy-start | bytes 4976644
  6.5 116.0 %all-gather.4.cloned.1.call-start = ((), (), s32[]{:S(2)}) async-start(), calls=%async_computation.5 | async-start | bytes 4456448 | tf_op jit(solution)/shard_map/all_gather | solution.py:91
  9.5 3.5 copy-start.2
  11.9 0.7 copy-start.16
  12.7 10.4 %copy-start.26 = (u32[128]{0:T(128)S(1)}, u32[128]{0:T(128)}, u32[]{:S(2)}) copy-start(u32[128]{0:T(128)} %constant.214) | copy-start | bytes 1540
  12.7 11.7 %copy-start.24 = (s32[8]{0:T(128)S(1)}, s32[8]{0:T(128)}, u32[]{:S(2)}) copy-start(s32[8]{0:T(128)} %param.31) | copy-start | bytes 100
  12.7 29.3 %copy-start.3 = (s32[8]{0:T(128)S(1)}, s32[8]{0:T(128)}, u32[]{:S(2)}) copy-start(s32[8]{0:T(128)} %param.33) | copy-start | bytes 100
  12.7 29.3 %copy-start.23 = (s32[2]{0:T(128)S(1)}, s32[2]{0:T(128)}, u32[]{:S(2)}) copy-start(s32[2]{0:T(128)} %param.30) | copy-start | bytes 28
  14.0 33.2 %copy-start.6 = (bf16[256,2304]{1,0:T(8,128)(2,1)S(1)}, bf16[256,2304]{1,0:T(8,128)(2,1)}, u32[]{:S(2)}) copy-start(bf16[256,2304]{1,0:T(8,128)(2,1)} %param.20) | copy-start | bytes 3538948
  14.9 47.3 %all-to-all-start = ((bf16[16,2,32,256]{3,2,1,0:T(8,128)(2,1)}), bf16[16,2,32,256]{3,2,1,0:T(8,128)(2,1)}, u32[]{:S(2)}, u32[]{:S(2)}) async-start(bf16[16,2,32,256]{3,2,1,0:T(8,128)(2,1)} %pad_maximum_fusion.1), calls=%async_computation | async-start | bytes 1048576 | tf_op jit(solution)/shard_map/all_to_all | solution.py:146
  44.9 4.7 %copy-start.7 = (bf16[2,2,1024,256]{3,2,1,0:T(8,128)(2,1)S(1)}, bf16[2,2,1024,256]{3,2,1,0:T(8,128)(2,1)}, u32[]{:S(2)}) copy-start(bf16[2,2,1024,256]{3,2,1,0:T(8,128)(2,1)} %param.28) | copy-start | bytes 6291460
  49.7 2.1 copy-start.19
  49.7 3.9 copy-start.9
  53.8 4.2 copy-start.10
  53.8 6.4 %copy-start.18 = (bf16[8,32,4,64]{3,2,1,0:T(4,128)(2,1)S(1)}, bf16[8,32,4,64]{3,2,1,0:T(4,128)(2,1)}, u32[]{:S(2)}) copy-start(bf16[8,32,4,64]{3,2,1,0:T(4,128)(2,1)} %reshape.404) | copy-start | bytes 393220
  68.9 2.7 copy-start.14
  68.9 2.7 copy-start.15
  78.9 2.0 copy-start.13
  82.8 2.5 copy-start.8
  87.6 6.6 %copy-start.25 = (f32[2304]{0:T(1024)S(1)}, f32[2304]{0:T(1024)}, u32[]{:S(2)}) copy-start(f32[2304]{0:T(1024)} %param.21) | copy-start | bytes 27652
  87.6 25.6 %all-to-all-start.1 = ((f32[16,2,32,260]{3,2,1,0:T(8,128)}), f32[16,2,32,260]{3,2,1,0:T(8,128)S(1)}, u32[]{:S(2)}, u32[]{:S(2)}) async-start(f32[16,2,32,260]{3,2,1,0:T(8,128)} %pad_maximum_fusion), calls=%async_computation.1 | async-start | bytes 3145728 | tf_op jit(solution)/shard_map/all_to_all | solution.py:164
  92.7 104.0 %reduce-scatter.4.cloned.1.call-start = ((), (), s32[]{:S(2)}) async-start(), calls=%async_computation.6 | async-start | bytes 2654208 | tf_op jit(solution)/shard_map/reduce_scatter | solution.py:180
  131.1 4.2 copy-start.17
  153.6 8.2 %copy-start.12 = (f32[1,256,4,64]{1,3,2,0:T(8,128)S(1)}, f32[1,256,4,64]{1,3,2,0:T(8,128)}, u32[]{:S(2)}) copy-start(f32[1,256,4,64]{1,3,2,0:T(8,128)} %copy.288) | copy-start | bytes 786436
  161.7 1.3 copy-start.11
  163.0 34.8 %copy-start.22 = (f32[2304]{0:T(1024)S(1)}, f32[2304]{0:T(1024)}, u32[]{:S(2)}) copy-start(f32[2304]{0:T(1024)} %param.34) | copy-start | bytes 27652
  164.9 34.8 %copy-start.21 = (s32[256,2]{0,1:T(2,128)S(1)}, s32[256,2]{0,1:T(2,128)}, u32[]{:S(2)}) copy-start(s32[256,2]{0,1:T(2,128)} %param.36) | copy-start | bytes 6148
  164.9 57.3 %all-gather.6.cloned.1.call-start = ((), (), s32[]{:S(2)}) async-start(), calls=%async_computation.7 | async-start | bytes 1327104 | tf_op jit(solution)/shard_map/all_gather | solution.py:183
  199.6 90.3 %all-gather.8.cloned.1.call-start = ((), (), s32[]{:S(2)}) async-start(), calls=%async_computation.8 | async-start | bytes 7520256 | tf_op jit(solution)/shard_map/all_gather | solution.py:203
  224.6 168.7 %reduce-scatter.6.cloned.1.call-start = ((), (), s32[]{:S(2)}) async-start(), calls=%async_computation.9 | async-start | bytes 7520256 | tf_op jit(solution)/shard_map/reduce_scatter | solution.py:211
  310.6 1.3 copy-start.4
  310.6 1.3 copy-start.20
  310.6 117.3 %reduce-scatter.8.cloned.1.call-start = ((), (), s32[]{:S(2)}) async-start(), calls=%async_computation.10 | async-start | bytes 1327104 | tf_op jit(solution)/shard_map/reduce_scatter | solution.py:216
  312.9 116.8 %copy-start.1 = (bf16[1,360,2304]{2,1,0:T(8,128)(2,1)S(1)}, bf16[1,360,2304]{2,1,0:T(8,128)(2,1)}, u32[]{:S(2)}) copy-start(bf16[1,360,2304]{2,1,0:T(8,128)(2,1)} %param.39) | copy-start | bytes 4976644
  316.4 111.5 %copy-start.5 = (f32[32,2304]{1,0:T(8,128)S(1)}, f32[32,2304]{1,0:T(8,128)}, u32[]{:S(2)}) copy-start(f32[32,2304]{1,0:T(8,128)} %reduce-scatter.4.cloned.1.call-done) | copy-start | bytes 884740
Sparse Core Ops, SparseCore 0:
  9.6 57.6 all-gather.3
  165.0 31.5 reduce-scatter.3
  199.7 22.4 all-gather.5
  224.7 65.1 all-gather.7
  310.8 82.4 reduce-scatter.5
  396.6 31.2 reduce-scatter.7
where the time goes:
time: 444 us; the launch traced here: 437 us
  waiting for transfers between devices  237 us (53%)
  matrix products  69.9 us (16%)
  local copies, waits for them, and re-layouts  55.5 us (12%)
  other arithmetic  27.1 us (6%)
  blocking collectives  17.4 us (4%)
  between operations  15.6 us (4%)
  starting transfers between devices  13.8 us (3%)
    reduce_scatter x1, waiting for transfers between devices, on_device(): lax.psum_scatter(partial_out.astype(jnp.bfloat16), 'dp', scatter_dimensio...  76.4 us
    all_gather x1, waiting for transfers between devices, on_device(): piece = lax.all_gather(dispatch, 'dp', axis=0, tiled=True)  65 us
    reduce_scatter x1, waiting for transfers between devices, on_device(): lax.psum_scatter(projected, 'mp', scatter_dimension=0, tiled=True)  31.7 us
    reduce_scatter x1, waiting for transfers between devices, on_device(): lax.psum_scatter(spread.astype(jnp.bfloat16), 'mp', scatter_dimension=0,...  30.7 us
    all_gather x1, waiting for transfers between devices, on_device(): ffn_in = lax.all_gather(ffn_rows, 'mp', axis=0, tiled=True)  21.9 us
    unnamed x1, blocking collectives  17.4 us
    dot_general x1, matrix products, on_device(): jnp.dot((jax.nn.silu(gate_part) * up_part).astype(jnp.bfloat16), down_wei...  13.1 us
    unnamed x64, local copies, waits for them, and re-layouts  11.2 us
  transfers between devices with their start and end apart: 8, of which 6 were waited for; matrix products, arithmetic and copies ran while one was open for 18% of the time, Pallas kernels for 0%

commit v1 on v0

--- a/solution.py
+++ b/solution.py
@@ -8,6 +8,22 @@
 TOP = 2
 EPS = 1e-05
 NEGATIVE = -1e30
+
+
+def ring_gather(x, axis, dim):
+    ways, here, hop = (lax.axis_size(axis), lax.axis_index(axis), x.shape[dim])
+    dims = [n * ways if d == dim else n for d, n in enumerate(x.shape)]
+    full = lax.dynamic_update_slice_in_dim(jnp.zeros(dims, x.dtype), x, here * hop, axis=dim)
+    going_up = going_down = x
+    for far in range(1, ways // 2 + 1):
+        going_up = lax.ppermute(going_up, axis, [(d, (d + 1) % ways) for d in range(ways)])
+        full = lax.dynamic_update_slice_in_dim(full, going_up, (here - far) % ways * hop, axis=dim)
+        if 2 * far < ways:
+            going_down = lax.ppermute(going_down, axis, [(d, (d - 1) % ways) for d in range(ways)])
+            full = lax.dynamic_update_slice_in_dim(
+                full, going_down, (here + far) % ways * hop, axis=dim
+            )
+    return full
 
 
 def rms_scale(rows, gain):
@@ -200,7 +216,7 @@
     gate_weight = w_gate[0]
     up_weight = w_up[0]
     down_weight = w_down[0]
-    piece = lax.all_gather(dispatch, "dp", axis=0, tiled=True)
+    piece = ring_gather(dispatch, "dp", 0)
     gate_part = jnp.dot(piece, gate_weight, preferred_element_type=jnp.float32)
     up_part = jnp.dot(piece, up_weight, preferred_element_type=jnp.float32)
     partial_out = jnp.dot(

time: 444 us -> 490 us (1.10)
  starting transfers between devices: 13.8 us -> 50 us
  local copies, waits for them, and re-layouts: 55.5 us -> 73.3 us
  waiting for transfers between devices: 237 us -> 224 us
    all_gather x1 -> x0, waiting for transfers between devices: 65 us -> none  [on_device(): piece = lax.all_gather(dispatch, 'dp', axis=0, tiled=True)]
    ppermute x0 -> x15, waiting for transfers between devices: none -> 55.7 us  [the longest x8 55.7 us: ring_gather(): lax.ppermute(going_up, axis, [(d, (d + 1) % ways) for d in range(ways)])]
    ppermute x0 -> x15, starting transfers between devices: none -> 37.7 us  [the longest x7 36.1 us: ring_gather(): lax.ppermute(going_down, axis, [(d, (d - 1) % ways) for d in range(ways)])]
    dynamic_update_slice x0 -> x15, local copies, waits for them, and re-layouts: none -> 13 us  [the longest x8 7.39 us: ring_gather(): lax.dynamic_update_slice_in_dim(full, going_up, (here - far) % ways * hop...]
    unnamed x64 -> x62, local copies, waits for them, and re-layouts: 11.2 us -> 10.8 us
  transfers between devices with their start and end apart: 8 -> 22, of which waited for: 6 -> 13; matrix products, arithmetic and copies ran while one was open for 18% -> 18% of each run, Pallas kernels for 0% -> 0%
where the time goes in v1:
time: 490 us; the launch traced here: 482 us
  waiting for transfers between devices  224 us (46%)
  matrix products  73.7 us (15%)
  local copies, waits for them, and re-layouts  73.3 us (15%)
  starting transfers between devices  50 us (10%)
  other arithmetic  28.3 us (6%)
  blocking collectives  16.9 us (3%)
  between operations  15.3 us (3%)
    reduce_scatter x1, waiting for transfers between devices, on_device(): lax.psum_scatter(partial_out.astype(jnp.bfloat16), 'dp', scatter_dimensio...  72.4 us
    ppermute x8, waiting for transfers between devices, ring_gather(): lax.ppermute(going_up, axis, [(d, (d + 1) % ways) for d in range(ways)])  55.7 us
    ppermute x7, starting transfers between devices, ring_gather(): lax.ppermute(going_down, axis, [(d, (d - 1) % ways) for d in range(ways)])  36.1 us
    reduce_scatter x1, waiting for transfers between devices, on_device(): lax.psum_scatter(projected, 'mp', scatter_dimension=0, tiled=True)  31.9 us
    reduce_scatter x1, waiting for transfers between devices, on_device(): lax.psum_scatter(spread.astype(jnp.bfloat16), 'mp', scatter_dimension=0,...  30.7 us
    all_gather x1, waiting for transfers between devices, on_device(): ffn_in = lax.all_gather(ffn_rows, 'mp', axis=0, tiled=True)  21.9 us
    unnamed x1, blocking collectives  16.9 us
    dot_general x1, matrix products, on_device(): jnp.dot((jax.nn.silu(gate_part) * up_part).astype(jnp.bfloat16), down_wei...  13.2 us
  transfers between devices with their start and end apart: 22, of which 13 were waited for; matrix products, arithmetic and copies ran while one was open for 18% of the time, Pallas kernels for 0%

profile of v1, /device:TPU:0, one launch (start us, length us, event | category | flops | bytes accessed | tf_op | source)
XLA Modules:
  0.0 481.8 jit_solution(11550363277348511779)
XLA Ops:
  8.3 2.4 convolution_convert_fusion.7
  14.9 8.1 %all-to-all-start = ((bf16[16,2,32,256]{3,2,1,0:T(8,128)(2,1)}), bf16[16,2,32,256]{3,2,1,0:T(8,128)(2,1)S(1)}, u32[]{:S(2)}, u32[]{:S(2)}) async-start(bf16[16,2,32,256]{3,2,1,0:T(8,128)(2,1)} %pad_maximum_fusion.1), calls=%async_computation | async-start | bytes 1048576 | tf_op jit(solution)/shard_map/all_to_all | solution.py:162
  25.3 16.9 %all-reduce.2 = s32[128]{0:T(128)S(1)} all-reduce(s32[128]{0:T(128)S(1)} %dynamic-update-slice), channel_id=1, replica_groups=mesh['dp'=16,'mp'=8] {'dp'}, use_global_device_ids=true, to_apply=%add.2 | all-reduce | flops 128 | bytes 1024
  45.1 2.2 fusion.128
  47.4 2.5 convolution_convert_fusion.6
  52.0 2.1 copy.296
  56.4 2.1 copy.294
  58.5 2.1 copy.295
  61.9 2.0 fusion.131
  67.5 2.9 bitcast_reduce_fusion.1
  70.8 2.5 fusion.13
  73.2 2.1 fusion.15
  76.5 5.4 %fusion.60 = f32[16,32,4,64]{3,1,2,0:T(8,128)S(1)} fusion(f32[16,4,1024,32]{2,3,1,0:T(8,128)} %copy-done.3, f32[16,32,4]{1,2,0:T(4,128)S(1)} %get-tuple-element.28, pred[16,1024]{1,0:T(8,128)(4,1)S(1)} %iota_compare_fusion.1, pred[16]{0:T(512)(128)(4,1)S(1)} %fusion.99, bf16[1024,4,64]{0,2,1:T(8,128)(2,1)S(1)} %bitcast.189, ...), kind=kOutput, calls=%fused_computation.74 | convolution fusion | flops 281149440 | bytes 9994256 | tf_op jit(solution)/shard_map/sqhk,skhd->sqhd/dot_general | solution.py:61
  83.3 4.7 fusion.65
  90.1 2.5 pad_maximum_fusion
  92.6 3.7 all-to-all-start.1
  97.7 2.8 convolution_convert_fusion.5
  105.8 11.0 %all-to-all-done.1 = f32[16,2,32,260]{3,2,1,0:T(8,128)S(1)} async-done(((f32[16,2,32,260]{3,2,1,0:T(8,128)}), f32[16,2,32,260]{3,2,1,0:T(8,128)S(1)}, u32[]{:S(2)}, u32[]{:S(2)}) %all-to-all-start.1) | async-done | bytes 1064992 | tf_op jit(solution)/shard_map/all_to_all | solution.py:180
  126.8 4.4 fusion.126
  131.2 4.3 copy.253
  135.6 9.7 %bitcast_reduce_fusion = (f32[256,4]{0,1:T(4,128)S(1)}, f32[4,256,4096]{2,1,0:T(8,128)}) fusion(bf16[256,4,64]{0,2,1:T(8,128)(2,1)S(1)} %bitcast.192, bf16[4096,4,64]{0,2,1:T(8,128)(2,1)} %bitcast.176), kind=kOutput, calls=%fused_computation.8 | convolution fusion | flops 545258496 | bytes 19009536 | tf_op jit(solution)/shard_map/qhd,khd->qhk/dot_general | solution.py:112
  145.3 4.2 copy.282
  149.4 8.6 %fusion.2 = f32[256,4]{0,1:T(4,128)S(1)} fusion(f32[4,256,4096]{2,1,0:T(8,128)} %get-tuple-element.33, f32[256,4]{0,1:T(4,128)S(1)} %broadcast_maximum_fusion), kind=kLoop, calls=%fused_computation.11 | loop fusion | flops 12581888 | bytes 16785408 | tf_op jit(solution)/shard_map/reduce_sum | solution.py:117
  158.1 10.2 %fusion.56 = f32[1,256,4,64]{1,3,2,0:T(8,128)} fusion(bf16[4096,4,64]{0,2,1:T(8,128)(2,1)} %bitcast.178, f32[4,256,4096]{2,1,0:T(8,128)} %get-tuple-element.33, f32[256,4]{0,1:T(4,128)S(1)} %broadcast_maximum_fusion, f32[256,4]{0,1:T(4,128)S(1)} %fusion.2), kind=kOutput, calls=%fused_computation.71 | convolution fusion | flops 549519360 | bytes 19144704 | tf_op jit(solution)/shard_map/qhk,khd->qhd/dot_general | solution.py:118
  171.6 31.9 %reduce-scatter.4.cloned.1.call-done = f32[32,2304]{1,0:T(8,128)} async-done(((f32[256,2304]{1,0:T(8,128)}), f32[32,2304]{1,0:T(8,128)}) %reduce-scatter.4.cloned.1.call-update) | async-done | bytes 294928 | tf_op jit(solution)/shard_map/reduce_scatter | solution.py:196
  207.2 21.9 %all-gather.5.cloned.1.call-done = bf16[256,2304]{1,0:T(8,128)(2,1)} async-done(((bf16[32,2304]{1,0:T(8,128)(2,1)}), bf16[256,2304]{1,0:T(8,128)(2,1)}) %all-gather.5.cloned.1.call-update) | async-done | bytes 1179664 | tf_op jit(solution)/shard_map/all_gather | solution.py:199
  229.0 3.4 broadcast_in_dim.179
  235.2 3.8 collective-permute-start.1
  239.0 10.7 %collective-permute-done = bf16[96,2304]{1,0:T(8,128)(2,1)} collective-permute-done((bf16[96,2304]{1,0:T(8,128)(2,1)}, bf16[96,2304]{1,0:T(8,128)(2,1)}, u32[]{:S(2)}, u32[]{:S(2)}) %collective-permute-start) | collective-permute-done | bytes 442400 | tf_op jit(solution)/shard_map/ppermute | solution.py:19
  249.7 5.6 %collective-permute-start.3 = (bf16[96,2304]{1,0:T(8,128)(2,1)S(1)}, bf16[96,2304]{1,0:T(8,128)(2,1)S(1)}, u32[]{:S(2)}, u32[]{:S(2)}) collective-permute-start(bf16[96,2304]{1,0:T(8,128)(2,1)S(1)} %collective-permute-done.1), channel_id=1, source_target_pairs={{0,120},{8,0},{16,8},{24,16},{32,24},{40,32},{48,40},{56,48},{64,5... | collective-permute-start | bytes 1327112 | tf_op jit(solution)/shard_map/ppermute | solution.py:22
  257.9 6.9 %collective-permute-done.2 = bf16[96,2304]{1,0:T(8,128)(2,1)S(1)} collective-permute-done((bf16[96,2304]{1,0:T(8,128)(2,1)}, bf16[96,2304]{1,0:T(8,128)(2,1)S(1)}, u32[]{:S(2)}, u32[]{:S(2)}) %collective-permute-start.2) | collective-permute-done | bytes 442400 | tf_op jit(solution)/shard_map/ppermute | solution.py:19
  264.8 5.3 %collective-permute-start.5 = (bf16[96,2304]{1,0:T(8,128)(2,1)S(1)}, bf16[96,2304]{1,0:T(8,128)(2,1)S(1)}, u32[]{:S(2)}, u32[]{:S(2)}) collective-permute-start(bf16[96,2304]{1,0:T(8,128)(2,1)S(1)} %collective-permute-done.3), channel_id=1, source_target_pairs={{0,120},{8,0},{16,8},{24,16},{32,24},{40,32},{48,40},{56,48},{64,5... | collective-permute-start | bytes 1327112 | tf_op jit(solution)/shard_map/ppermute | solution.py:22
  271.7 7.0 %collective-permute-done.4 = bf16[96,2304]{1,0:T(8,128)(2,1)S(1)} collective-permute-done((bf16[96,2304]{1,0:T(8,128)(2,1)S(1)}, bf16[96,2304]{1,0:T(8,128)(2,1)S(1)}, u32[]{:S(2)}, u32[]{:S(2)}) %collective-permute-start.4) | collective-permute-done | bytes 442400 | tf_op jit(solution)/shard_map/ppermute | solution.py:19
  278.7 5.3 %collective-permute-start.7 = (bf16[96,2304]{1,0:T(8,128)(2,1)S(1)}, bf16[96,2304]{1,0:T(8,128)(2,1)S(1)}, u32[]{:S(2)}, u32[]{:S(2)}) collective-permute-start(bf16[96,2304]{1,0:T(8,128)(2,1)S(1)} %collective-permute-done.5), channel_id=1, source_target_pairs={{0,120},{8,0},{16,8},{24,16},{32,24},{40,32},{48,40},{56,48},{64,5... | collective-permute-start | bytes 1327112 | tf_op jit(solution)/shard_map/ppermute | solution.py:22
  285.7 6.1 %collective-permute-done.6 = bf16[96,2304]{1,0:T(8,128)(2,1)S(1)} collective-permute-done((bf16[96,2304]{1,0:T(8,128)(2,1)S(1)}, bf16[96,2304]{1,0:T(8,128)(2,1)S(1)}, u32[]{:S(2)}, u32[]{:S(2)}) %collective-permute-start.6) | collective-permute-done | bytes 442400 | tf_op jit(solution)/shard_map/ppermute | solution.py:19
  291.8 5.3 %collective-permute-start.9 = (bf16[96,2304]{1,0:T(8,128)(2,1)S(1)}, bf16[96,2304]{1,0:T(8,128)(2,1)S(1)}, u32[]{:S(2)}, u32[]{:S(2)}) collective-permute-start(bf16[96,2304]{1,0:T(8,128)(2,1)S(1)} %collective-permute-done.7), channel_id=1, source_target_pairs={{0,120},{8,0},{16,8},{24,16},{32,24},{40,32},{48,40},{56,48},{64,5... | collective-permute-start | bytes 1327112 | tf_op jit(solution)/shard_map/ppermute | solution.py:22
  298.7 5.1 %collective-permute-done.8 = bf16[96,2304]{1,0:T(8,128)(2,1)S(1)} collective-permute-done((bf16[96,2304]{1,0:T(8,128)(2,1)S(1)}, bf16[96,2304]{1,0:T(8,128)(2,1)S(1)}, u32[]{:S(2)}, u32[]{:S(2)}) %collective-permute-start.8) | collective-permute-done | bytes 442400 | tf_op jit(solution)/shard_map/ppermute | solution.py:19
  303.9 5.3 %collective-permute-start.11 = (bf16[96,2304]{1,0:T(8,128)(2,1)S(1)}, bf16[96,2304]{1,0:T(8,128)(2,1)S(1)}, u32[]{:S(2)}, u32[]{:S(2)}) collective-permute-start(bf16[96,2304]{1,0:T(8,128)(2,1)S(1)} %collective-permute-done.9), channel_id=1, source_target_pairs={{0,120},{8,0},{16,8},{24,16},{32,24},{40,32},{48,40},{56,48},{64,5... | collective-permute-start | bytes 1327112 | tf_op jit(solution)/shard_map/ppermute | solution.py:22
  310.8 4.7 collective-permute-done.10
  315.5 5.3 %collective-permute-start.13 = (bf16[96,2304]{1,0:T(8,128)(2,1)S(1)}, bf16[96,2304]{1,0:T(8,128)(2,1)S(1)}, u32[]{:S(2)}, u32[]{:S(2)}) collective-permute-start(bf16[96,2304]{1,0:T(8,128)(2,1)S(1)} %collective-permute-done.11), channel_id=1, source_target_pairs={{0,120},{8,0},{16,8},{24,16},{32,24},{40,32},{48,40},{56,48},{64,5... | collective-permute-start | bytes 1327112 | tf_op jit(solution)/shard_map/ppermute | solution.py:22
  322.5 5.2 %collective-permute-done.12 = bf16[96,2304]{1,0:T(8,128)(2,1)S(1)} collective-permute-done((bf16[96,2304]{1,0:T(8,128)(2,1)S(1)}, bf16[96,2304]{1,0:T(8,128)(2,1)S(1)}, u32[]{:S(2)}, u32[]{:S(2)}) %collective-permute-start.12) | collective-permute-done | bytes 442400 | tf_op jit(solution)/shard_map/ppermute | solution.py:19
  329.2 10.0 %collective-permute-done.14 = bf16[96,2304]{1,0:T(8,128)(2,1)S(1)} collective-permute-done((bf16[96,2304]{1,0:T(8,128)(2,1)S(1)}, bf16[96,2304]{1,0:T(8,128)(2,1)S(1)}, u32[]{:S(2)}, u32[]{:S(2)}) %collective-permute-start.14) | collective-permute-done | bytes 442400 | tf_op jit(solution)/shard_map/ppermute | solution.py:19
  340.1 7.2 %fusion.37 = f32[1536,360]{0,1:T(8,128)} fusion(bf16[1536,2304]{1,0:T(8,128)(2,1)} %constant_dynamic-update-slice_fusion, bf16[1,2304,360]{1,2,0:T(8,128)(2,1)S(1)} %copy-done.23), kind=kOutput, calls=%fused_computation.55 | convolution fusion | flops 2548039680 | bytes 10948608 | tf_op jit(solution)/shard_map/dot_general | solution.py:220
  347.2 13.2 %convolution_convert_fusion = bf16[1536,2304]{1,0:T(8,128)(2,1)} fusion(bf16[1,360,2304]{2,1,0:T(8,128)(2,1)S(1)} %copy-done, f32[1536,360]{0,1:T(8,128)} %fusion.37, bf16[1536,2304]{1,0:T(8,128)(2,1)} %constant_dynamic-update-slice_fusion, bf16[1,2304,360]{1,2,0:T(8,128)(2,1)} %param.38), kind=kOutput, calls=%fused_computation.12 | convolution fusion | flops 5102936064 | bytes 19685376 | tf_op jit(solution)/shard_map/dot_general | solution.py:222
  362.3 3.6 gather_fusion.6
  366.3 72.4 %reduce-scatter.6.cloned.1.call-done = bf16[96,2304]{1,0:T(8,128)(2,1)} async-done(((bf16[1536,2304]{1,0:T(8,128)(2,1)}), bf16[96,2304]{1,0:T(8,128)(2,1)}) %reduce-scatter.6.cloned.1.call-update) | async-done | bytes 442384 | tf_op jit(solution)/shard_map/reduce_scatter | solution.py:227
  438.6 3.2 convolution_convert_fusion.3
  442.6 30.7 %reduce-scatter.8.cloned.1.call-done = bf16[32,2304]{1,0:T(8,128)(2,1)} async-done(((bf16[256,2304]{1,0:T(8,128)(2,1)}), bf16[32,2304]{1,0:T(8,128)(2,1)}) %reduce-scatter.8.cloned.1.call-update) | async-done | bytes 147472 | tf_op jit(solution)/shard_map/reduce_scatter | solution.py:232
  (192 shorter events, 67.8 us)
Async XLA Ops:
  6.5 340.7 %copy-start = (bf16[1,360,2304]{2,1,0:T(8,128)(2,1)S(1)}, bf16[1,360,2304]{2,1,0:T(8,128)(2,1)}, u32[]{:S(2)}) copy-start(bf16[1,360,2304]{2,1,0:T(8,128)(2,1)} %param.39) | copy-start | bytes 4976644
  6.5 17.2 %copy-start.25 = (u32[128]{0:T(128)S(1)}, u32[128]{0:T(128)}, u32[]{:S(2)}) copy-start(u32[128]{0:T(128)} %constant.312) | copy-start | bytes 1540
  6.5 40.8 %copy-start.6 = (bf16[256,2304]{1,0:T(8,128)(2,1)S(1)}, bf16[256,2304]{1,0:T(8,128)(2,1)}, u32[]{:S(2)}) copy-start(bf16[256,2304]{1,0:T(8,128)(2,1)} %param.20) | copy-start | bytes 3538948
  6.5 18.5 %copy-start.22 = (s32[8]{0:T(128)S(1)}, s32[8]{0:T(128)}, u32[]{:S(2)}) copy-start(s32[8]{0:T(128)} %param.31) | copy-start | bytes 100
  6.5 35.8 %copy-start.21 = (s32[2]{0:T(128)S(1)}, s32[2]{0:T(128)}, u32[]{:S(2)}) copy-start(s32[2]{0:T(128)} %param.30) | copy-start | bytes 28
  6.5 36.4 %copy-start.1 = (s32[8]{0:T(128)S(1)}, s32[8]{0:T(128)}, u32[]{:S(2)}) copy-start(s32[8]{0:T(128)} %param.33) | copy-start | bytes 100
  10.7 0.7 copy-start.15
  14.9 49.1 %all-to-all-start = ((bf16[16,2,32,256]{3,2,1,0:T(8,128)(2,1)}), bf16[16,2,32,256]{3,2,1,0:T(8,128)(2,1)S(1)}, u32[]{:S(2)}, u32[]{:S(2)}) async-start(bf16[16,2,32,256]{3,2,1,0:T(8,128)(2,1)} %pad_maximum_fusion.1), calls=%async_computation | async-start | bytes 1048576 | tf_op jit(solution)/shard_map/all_to_all | solution.py:162
  23.0 103.8 %all-gather.3.cloned.1.call-start = ((), (), s32[]{:S(2)}) async-start(), calls=%async_computation.5 | async-start | bytes 4456448 | tf_op jit(solution)/shard_map/all_gather | solution.py:107
  42.3 7.6 %copy-start.7 = (bf16[2,2,1024,256]{3,2,1,0:T(8,128)(2,1)S(1)}, bf16[2,2,1024,256]{3,2,1,0:T(8,128)(2,1)}, u32[]{:S(2)}) copy-start(bf16[2,2,1024,256]{3,2,1,0:T(8,128)(2,1)} %param.28) | copy-start | bytes 6291460
  49.9 10.7 %copy-start.8 = (bf16[1,1,1024,256]{3,2,1,0:T(8,128)(2,1)S(1)}, bf16[1,1,1024,256]{3,2,1,0:T(8,128)(2,1)}, u32[]{:S(2)}) copy-start(bf16[1,1,1024,256]{3,2,1,0:T(8,128)(2,1)} %get-tuple-element.17) | copy-start | bytes 1572868
  49.9 11.8 %copy-start.17 = (bf16[256,256]{1,0:T(8,128)(2,1)S(1)}, bf16[256,256]{1,0:T(8,128)(2,1)}, u32[]{:S(2)}) copy-start(bf16[256,256]{1,0:T(8,128)(2,1)} %convolution_convert_fusion.6) | copy-start | bytes 393220
  66.2 1.4 copy-start.13
  66.2 1.4 copy-start.14
  67.5 3.2 copy-start.2
  70.5 4.9 %copy-start.3 = (f32[16,4,1024,32]{2,3,1,0:T(8,128)}, f32[16,4,1024,32]{2,3,1,0:T(8,128)S(1)}, u32[]{:S(2)}) copy-start(f32[16,4,1024,32]{2,3,1,0:T(8,128)S(1)} %get-tuple-element.29) | copy-start | bytes 25165828
  70.7 5.7 %copy-start.11 = (bf16[1,1,1024,256]{2,3,1,0:T(8,128)(2,1)S(1)}, bf16[1,1,1024,256]{2,3,1,0:T(8,128)(2,1)}, u32[]{:S(2)}) copy-start(bf16[1,1,1024,256]{2,3,1,0:T(8,128)(2,1)} %copy.294) | copy-start | bytes 1572868
  70.7 5.7 %copy-start.12 = (bf16[1,1,1024,256]{2,3,1,0:T(8,128)(2,1)S(1)}, bf16[1,1,1024,256]{2,3,1,0:T(8,128)(2,1)}, u32[]{:S(2)}) copy-start(bf16[1,1,1024,256]{2,3,1,0:T(8,128)(2,1)} %copy.295) | copy-start | bytes 1572868
  88.0 9.8 %copy-start.24 = (f32[2304]{0:T(1024)S(1)}, f32[2304]{0:T(1024)}, u32[]{:S(2)}) copy-start(f32[2304]{0:T(1024)} %param.21) | copy-start | bytes 27652
  92.6 24.2 %all-to-all-start.1 = ((f32[16,2,32,260]{3,2,1,0:T(8,128)}), f32[16,2,32,260]{3,2,1,0:T(8,128)S(1)}, u32[]{:S(2)}, u32[]{:S(2)}) async-start(f32[16,2,32,260]{3,2,1,0:T(8,128)} %pad_maximum_fusion), calls=%async_computation.1 | async-start | bytes 3145728 | tf_op jit(solution)/shard_map/all_to_all | solution.py:180
  96.3 107.2 %reduce-scatter.4.cloned.1.call-start = ((), (), s32[]{:S(2)}) async-start(), calls=%async_computation.6 | async-start | bytes 2654208 | tf_op jit(solution)/shard_map/reduce_scatter | solution.py:196
  125.6 9.9 %copy-start.16 = (bf16[256,256]{0,1:T(8,128)(2,1)S(1)}, bf16[256,256]{0,1:T(8,128)(2,1)}, u32[]{:S(2)}) copy-start(bf16[256,256]{0,1:T(8,128)(2,1)} %copy-done.15) | copy-start | bytes 393220
  158.1 10.3 %copy-start.10 = (f32[1,256,4,64]{1,3,2,0:T(8,128)S(1)}, f32[1,256,4,64]{1,3,2,0:T(8,128)}, u32[]{:S(2)}) copy-start(f32[1,256,4,64]{1,3,2,0:T(8,128)} %copy.288) | copy-start | bytes 786436
  158.1 11.5 %copy-start.9 = (bf16[256,2304]{1,0:T(8,128)(2,1)S(1)}, bf16[256,2304]{1,0:T(8,128)(2,1)}, u32[]{:S(2)}) copy-start(bf16[256,2304]{1,0:T(8,128)(2,1)} %param.25) | copy-start | bytes 3538948
  168.3 36.4 %copy-start.20 = (f32[2304]{0:T(1024)S(1)}, f32[2304]{0:T(1024)}, u32[]{:S(2)}) copy-start(f32[2304]{0:T(1024)} %param.34) | copy-start | bytes 27652
  168.3 38.2 %copy-start.19 = (s32[256,2]{0,1:T(2,128)S(1)}, s32[256,2]{0,1:T(2,128)}, u32[]{:S(2)}) copy-start(s32[256,2]{0,1:T(2,128)} %param.36) | copy-start | bytes 6148
  171.6 57.5 %all-gather.5.cloned.1.call-start = ((), (), s32[]{:S(2)}) async-start(), calls=%async_computation.7 | async-start | bytes 1327104 | tf_op jit(solution)/shard_map/all_gather | solution.py:199
  206.5 232.2 %reduce-scatter.6.cloned.1.call-start = ((), (), s32[]{:S(2)}) async-start(), calls=%async_computation.8 | async-start | bytes 7520256 | tf_op jit(solution)/shard_map/reduce_scatter | solution.py:227
  229.0 3.4 copy-start.4
  233.7 16.0 %collective-permute-start = (bf16[96,2304]{1,0:T(8,128)(2,1)}, bf16[96,2304]{1,0:T(8,128)(2,1)}, u32[]{:S(2)}, u32[]{:S(2)}) collective-permute-start(bf16[96,2304]{1,0:T(8,128)(2,1)} %get-tuple-element.35), channel_id=1, source_target_pairs={{0,8},{8,16},{16,24},{24,32},{32,40},{40,48},{48,56},{56,64},{64,7... | collective-permute-start | bytes 1327112 | tf_op jit(solution)/shard_map/ppermute | solution.py:19
  235.2 14.4 %collective-permute-start.1 = (bf16[96,2304]{1,0:T(8,128)(2,1)}, bf16[96,2304]{1,0:T(8,128)(2,1)S(1)}, u32[]{:S(2)}, u32[]{:S(2)}) collective-permute-start(bf16[96,2304]{1,0:T(8,128)(2,1)} %get-tuple-element.35), channel_id=1, source_target_pairs={{0,120},{8,0},{16,8},{24,16},{32,24},{40,32},{48,40},{56,48},{64,5... | collective-permute-start | bytes 1327112 | tf_op jit(solution)/shard_map/ppermute | solution.py:22
  239.0 101.0 %copy-start.23 = (bf16[1,2304,360]{1,2,0:T(8,128)(2,1)S(1)}, bf16[1,2304,360]{1,2,0:T(8,128)(2,1)}, u32[]{:S(2)}) copy-start(bf16[1,2304,360]{1,2,0:T(8,128)(2,1)} %param.37) | copy-start | bytes 4976644
  249.7 15.1 %collective-permute-start.2 = (bf16[96,2304]{1,0:T(8,128)(2,1)}, bf16[96,2304]{1,0:T(8,128)(2,1)S(1)}, u32[]{:S(2)}, u32[]{:S(2)}) collective-permute-start(bf16[96,2304]{1,0:T(8,128)(2,1)} %collective-permute-done), channel_id=1, source_target_pairs={{0,8},{8,16},{16,24},{24,32},{32,40},{40,48},{48,56},{56,64},{64,7... | collective-permute-start | bytes 1327112 | tf_op jit(solution)/shard_map/ppermute | solution.py:19
  249.7 15.1 %collective-permute-start.3 = (bf16[96,2304]{1,0:T(8,128)(2,1)S(1)}, bf16[96,2304]{1,0:T(8,128)(2,1)S(1)}, u32[]{:S(2)}, u32[]{:S(2)}) collective-permute-start(bf16[96,2304]{1,0:T(8,128)(2,1)S(1)} %collective-permute-done.1), channel_id=1, source_target_pairs={{0,120},{8,0},{16,8},{24,16},{32,24},{40,32},{48,40},{56,48},{64,5... | collective-permute-start | bytes 1327112 | tf_op jit(solution)/shard_map/ppermute | solution.py:22
  264.8 14.0 %collective-permute-start.4 = (bf16[96,2304]{1,0:T(8,128)(2,1)S(1)}, bf16[96,2304]{1,0:T(8,128)(2,1)S(1)}, u32[]{:S(2)}, u32[]{:S(2)}) collective-permute-start(bf16[96,2304]{1,0:T(8,128)(2,1)S(1)} %collective-permute-done.2), channel_id=1, source_target_pairs={{0,8},{8,16},{16,24},{24,32},{32,40},{40,48},{48,56},{56,64},{64,7... | collective-permute-start | bytes 1327112 | tf_op jit(solution)/shard_map/ppermute | solution.py:19
  264.8 14.0 %collective-permute-start.5 = (bf16[96,2304]{1,0:T(8,128)(2,1)S(1)}, bf16[96,2304]{1,0:T(8,128)(2,1)S(1)}, u32[]{:S(2)}, u32[]{:S(2)}) collective-permute-start(bf16[96,2304]{1,0:T(8,128)(2,1)S(1)} %collective-permute-done.3), channel_id=1, source_target_pairs={{0,120},{8,0},{16,8},{24,16},{32,24},{40,32},{48,40},{56,48},{64,5... | collective-permute-start | bytes 1327112 | tf_op jit(solution)/shard_map/ppermute | solution.py:22
  278.7 13.0 %collective-permute-start.6 = (bf16[96,2304]{1,0:T(8,128)(2,1)S(1)}, bf16[96,2304]{1,0:T(8,128)(2,1)S(1)}, u32[]{:S(2)}, u32[]{:S(2)}) collective-permute-start(bf16[96,2304]{1,0:T(8,128)(2,1)S(1)} %collective-permute-done.4), channel_id=1, source_target_pairs={{0,8},{8,16},{16,24},{24,32},{32,40},{40,48},{48,56},{56,64},{64,7... | collective-permute-start | bytes 1327112 | tf_op jit(solution)/shard_map/ppermute | solution.py:19
  278.7 13.0 %collective-permute-start.7 = (bf16[96,2304]{1,0:T(8,128)(2,1)S(1)}, bf16[96,2304]{1,0:T(8,128)(2,1)S(1)}, u32[]{:S(2)}, u32[]{:S(2)}) collective-permute-start(bf16[96,2304]{1,0:T(8,128)(2,1)S(1)} %collective-permute-done.5), channel_id=1, source_target_pairs={{0,120},{8,0},{16,8},{24,16},{32,24},{40,32},{48,40},{56,48},{64,5... | collective-permute-start | bytes 1327112 | tf_op jit(solution)/shard_map/ppermute | solution.py:22
  291.8 12.1 %collective-permute-start.8 = (bf16[96,2304]{1,0:T(8,128)(2,1)S(1)}, bf16[96,2304]{1,0:T(8,128)(2,1)S(1)}, u32[]{:S(2)}, u32[]{:S(2)}) collective-permute-start(bf16[96,2304]{1,0:T(8,128)(2,1)S(1)} %collective-permute-done.6), channel_id=1, source_target_pairs={{0,8},{8,16},{16,24},{24,32},{32,40},{40,48},{48,56},{56,64},{64,7... | collective-permute-start | bytes 1327112 | tf_op jit(solution)/shard_map/ppermute | solution.py:19
  291.8 12.1 %collective-permute-start.9 = (bf16[96,2304]{1,0:T(8,128)(2,1)S(1)}, bf16[96,2304]{1,0:T(8,128)(2,1)S(1)}, u32[]{:S(2)}, u32[]{:S(2)}) collective-permute-start(bf16[96,2304]{1,0:T(8,128)(2,1)S(1)} %collective-permute-done.7), channel_id=1, source_target_pairs={{0,120},{8,0},{16,8},{24,16},{32,24},{40,32},{48,40},{56,48},{64,5... | collective-permute-start | bytes 1327112 | tf_op jit(solution)/shard_map/ppermute | solution.py:22
  303.9 11.6 %collective-permute-start.10 = (bf16[96,2304]{1,0:T(8,128)(2,1)S(1)}, bf16[96,2304]{1,0:T(8,128)(2,1)S(1)}, u32[]{:S(2)}, u32[]{:S(2)}) collective-permute-start(bf16[96,2304]{1,0:T(8,128)(2,1)S(1)} %collective-permute-done.8), channel_id=1, source_target_pairs={{0,8},{8,16},{16,24},{24,32},{32,40},{40,48},{48,56},{56,64},{64,7... | collective-permute-start | bytes 1327112 | tf_op jit(solution)/shard_map/ppermute | solution.py:19
  303.9 11.6 %collective-permute-start.11 = (bf16[96,2304]{1,0:T(8,128)(2,1)S(1)}, bf16[96,2304]{1,0:T(8,128)(2,1)S(1)}, u32[]{:S(2)}, u32[]{:S(2)}) collective-permute-start(bf16[96,2304]{1,0:T(8,128)(2,1)S(1)} %collective-permute-done.9), channel_id=1, source_target_pairs={{0,120},{8,0},{16,8},{24,16},{32,24},{40,32},{48,40},{56,48},{64,5... | collective-permute-start | bytes 1327112 | tf_op jit(solution)/shard_map/ppermute | solution.py:22
  315.5 12.1 %collective-permute-start.12 = (bf16[96,2304]{1,0:T(8,128)(2,1)S(1)}, bf16[96,2304]{1,0:T(8,128)(2,1)S(1)}, u32[]{:S(2)}, u32[]{:S(2)}) collective-permute-start(bf16[96,2304]{1,0:T(8,128)(2,1)S(1)} %collective-permute-done.10), channel_id=1, source_target_pairs={{0,8},{8,16},{16,24},{24,32},{32,40},{40,48},{48,56},{56,64},{64,7... | collective-permute-start | bytes 1327112 | tf_op jit(solution)/shard_map/ppermute | solution.py:19
  315.5 12.9 %collective-permute-start.13 = (bf16[96,2304]{1,0:T(8,128)(2,1)S(1)}, bf16[96,2304]{1,0:T(8,128)(2,1)S(1)}, u32[]{:S(2)}, u32[]{:S(2)}) collective-permute-start(bf16[96,2304]{1,0:T(8,128)(2,1)S(1)} %collective-permute-done.11), channel_id=1, source_target_pairs={{0,120},{8,0},{16,8},{24,16},{32,24},{40,32},{48,40},{56,48},{64,5... | collective-permute-start | bytes 1327112 | tf_op jit(solution)/shard_map/ppermute | solution.py:22
  327.6 11.6 %collective-permute-start.14 = (bf16[96,2304]{1,0:T(8,128)(2,1)S(1)}, bf16[96,2304]{1,0:T(8,128)(2,1)S(1)}, u32[]{:S(2)}, u32[]{:S(2)}) collective-permute-start(bf16[96,2304]{1,0:T(8,128)(2,1)S(1)} %collective-permute-done.12), channel_id=1, source_target_pairs={{0,8},{8,16},{16,24},{24,32},{32,40},{40,48},{48,56},{56,64},{64,7... | collective-permute-start | bytes 1327112 | tf_op jit(solution)/shard_map/ppermute | solution.py:19
  360.4 0.9 copy-start.18
  360.4 112.9 %reduce-scatter.8.cloned.1.call-start = ((), (), s32[]{:S(2)}) async-start(), calls=%async_computation.9 | async-start | bytes 1327104 | tf_op jit(solution)/shard_map/reduce_scatter | solution.py:232
  362.3 111.0 %copy-start.5 = (f32[32,2304]{1,0:T(8,128)S(1)}, f32[32,2304]{1,0:T(8,128)}, u32[]{:S(2)}) copy-start(f32[32,2304]{1,0:T(8,128)} %reduce-scatter.4.cloned.1.call-done) | copy-start | bytes 884740
Sparse Core Ops, SparseCore 0:
  26.1 53.2 all-gather.2
  171.7 31.7 reduce-scatter.3
  206.6 22.4 all-gather.4
  360.6 78.0 reduce-scatter.5
  442.0 31.2 reduce-scatter.7
